TPU v7x, 256 devices: a whole 4x4x8 slice. The times are simulated.
256 devices in a mesh: blk: 128 (over x, z, y_hi, core), panel: 2 (over y_lo).
Axes of the slice: x: 4, y: 4 (y_hi: 2, y_lo: 2; y = y_hi * 2 + y_lo), z: 8, core: 2. Of those that a mesh axis runs over, the one named last changes fastest.
Arguments:
- tiles: bfloat16 [131072, 2, 8, 256], P('blk', 'panel'), may hold values from -6 to 6
- loadings: float32 [131072, 512], P('blk'), may hold values from -6 to 6
- maps: float32 [128, 2, 256, 512], P('blk', 'panel'), may hold values from -6 to 6
- run_counts: int32 [512], P('blk'), may hold values from 64 to 256, as said below
Outputs:
- loadings_out: float32 [131072, 512], P(('blk', 'panel'))
- maps_after: float32 [128, 2, 256, 512], P('blk', 'panel')
Inputs may be any that keep to these rules, and one draw needn't show every extreme that they name: `run_counts`: valid frames at the start of each run of 256 frames; some run has all 256 valid and some only 64.
All inputs are finite; a program needn't handle non-finite values.
Results may differ from a plain program's by a relative error of at most 0.0028.
Values may be sent and summed in bfloat16 or wider, within the bound.
No kernel may reach another device: no remote copies, remote signals or barrier semaphores. Data moves between devices by JAX's collectives and lax.ppermute only.
A program may use at most 64 MiB of HBM per device.

v0:
```python
import jax
import jax.numpy as jnp
from jax import lax
from jax.sharding import PartitionSpec as P

RUN_LEN = 256
STEPS = 8


map_rate = 0.1
load_rate = 0.05


def shifted(array, axis, by):
    count = lax.axis_size(axis)
    return lax.ppermute(array, axis, [(i, (i + by) % count) for i in range(count)])


def split_up(array, dim, count):
    dims = array.shape
    parts = array.reshape(*dims[:dim], count, dims[dim] // count, *dims[dim + 1 :])
    return jnp.moveaxis(parts, dim, 0)


def summed_on_arrival(array, axis, dim):
    parts = split_up(array, dim, lax.axis_size(axis))
    arrived = lax.all_to_all(parts, axis, split_axis=0, concat_axis=0, tiled=True)
    return arrived.sum(axis=0)


def from_everyone(array, axis):
    copies = jnp.broadcast_to(array, (lax.axis_size(axis), *array.shape))
    return lax.all_to_all(copies, axis, split_axis=0, concat_axis=0, tiled=True)


def in_order(parts, dim):
    dims = list(parts.shape[1:])
    dims[dim] *= parts.shape[0]
    return jnp.moveaxis(parts, 0, dim).reshape(dims)


def collect(array, axis, dim):
    parts = from_everyone(array, axis)
    return in_order(parts, dim)


def per_device(tiles, loadings, maps, run_counts):
    frames = tiles.shape[0]
    rank = maps.shape[-1]
    scale = 1.0 / rank**0.5
    within = jnp.arange(frames, dtype=jnp.int32)
    limits = jnp.repeat(run_counts, RUN_LEN)
    mask = (within % RUN_LEN < limits).astype(jnp.float32)
    data = tiles[:, 0]
    current = maps[0, 0]
    half_rows = frames // 2
    start = lax.axis_index("panel") * half_rows
    own_rows = lax.dynamic_slice_in_dim(loadings, start, half_rows, 0)
    loads_bf = loadings.astype(jnp.bfloat16)
    half = STEPS // 2
    for part in range(2):
        acc = jnp.zeros((frames, rank), jnp.float32)
        for step in range(part * half, (part + 1) * half):
            block_bf = current.astype(jnp.bfloat16)
            prod = lax.dot_general(
                loads_bf, block_bf, (((1,), (1,)), ((), ())), preferred_element_type=jnp.float32
            )
            resid = ((data[:, step, :].astype(jnp.float32) - prod * scale) * mask[:, None]).astype(
                jnp.bfloat16
            )
            grad_map = lax.dot_general(
                resid, loads_bf, (((0,), (0,)), ((), ())), preferred_element_type=jnp.float32
            )
            acc = acc + jnp.dot(resid, block_bf, preferred_element_type=jnp.float32) * scale
            current = shifted(current + map_rate * scale * grad_map, "blk", 1)
        share = summed_on_arrival(acc, "panel", 0)
        own_rows = own_rows + load_rate * share
        if part == 0:
            loads_bf = collect(own_rows.astype(jnp.bfloat16), "panel", 0)
    return (own_rows, current.reshape(1, 1, current.shape[0], rank))


def solution(mesh):
    in_specs = (
        P("blk", "panel", None, None),
        P("blk", None),
        P("blk", "panel", None, None),
        P("blk"),
    )
    out_specs = (P(("blk", "panel"), None), P("blk", "panel", None, None))
    return jax.shard_map(
        per_device, mesh=mesh, in_specs=in_specs, out_specs=out_specs, check_vma=False
    )
```

profile of v0, /device:TPU:6, one launch (start us, length us, event | category | flops | bytes accessed | tf_op | source)
XLA Modules:
  0.0 187.3 jit_solution(8684782010178307581)
XLA Ops:
  0.7 3.2 %copy.15 = bf16[1024,1,8,256]{3,0,2,1:T(8,128)(2,1)S(1)} copy(bf16[1024,1,8,256]{3,2,1,0:T(8,128)(2,1)} %param.4) | data formatting | bytes 8388608 | tf_op args[0]
  3.9 0.1 convert_element_type.111
  4.1 1.2 copy-done.6
  5.3 0.5 fusion.19
  5.8 0.5 fusion.27
  6.3 15.0 %collective-permute-done = f32[256,512]{1,0:T(8,128)S(1)} collective-permute-done((f32[256,512]{1,0:T(8,128)S(1)}, f32[256,512]{1,0:T(8,128)S(1)}, u32[]{:S(2)}, u32[]{:S(2)}) %collective-permute-start) | collective-permute-done | bytes 524320 | tf_op jit(solution)/shard_map/ppermute | solution.py:16
  21.4 0.5 fusion.20
  21.9 0.5 fusion.28
  22.4 0.4 fusion.69
  22.9 12.7 %collective-permute-done.1 = f32[256,512]{1,0:T(8,128)S(1)} collective-permute-done((f32[256,512]{1,0:T(8,128)S(1)}, f32[256,512]{1,0:T(8,128)S(1)}, u32[]{:S(2)}, u32[]{:S(2)}) %collective-permute-start.1) | collective-permute-done | bytes 524320 | tf_op jit(solution)/shard_map/ppermute | solution.py:16
  35.5 0.5 fusion.21
  36.0 0.5 fusion.29
  36.6 0.4 fusion.59
  37.0 0.4 fusion.56
  37.4 12.2 %collective-permute-done.2 = f32[256,512]{1,0:T(8,128)S(1)} collective-permute-done((f32[256,512]{1,0:T(8,128)S(1)}, f32[256,512]{1,0:T(8,128)S(1)}, u32[]{:S(2)}, u32[]{:S(2)}) %collective-permute-start.2) | collective-permute-done | bytes 524320 | tf_op jit(solution)/shard_map/ppermute | solution.py:16
  49.7 0.5 fusion.22
  50.2 1.8 add_multiply_fusion.1
  52.0 4.8 %all-to-all-start = ((f32[2,512,512]{2,1,0:T(8,128)}), f32[2,512,512]{2,1,0:T(8,128)}, u32[]{:S(2)}, u32[]{:S(2)}) async-start(f32[2,512,512]{2,1,0:T(8,128)} %bitcast.137), calls=%async_computation | async-start | bytes 4194304 | tf_op jit(solution)/shard_map/all_to_all | solution.py:27
  56.8 2.5 %fusion.30 = f32[256,512]{1,0:T(8,128)} fusion(f32[256,512]{1,0:T(8,128)} %copy-done.4, bf16[1024,256]{1,0:T(8,128)(2,1)} %copy-done.5, bf16[1024,512]{1,0:T(8,128)(2,1)S(1)} %convert_element_type.111), kind=kOutput, calls=%fused_computation.49 | convolution fusion | flops 268697600 | bytes 2621440 | tf_op jit(solution)/shard_map/dot_general | solution.py:71
  59.3 22.9 %all-to-all-done = f32[2,512,512]{2,1,0:T(8,128)} async-done(((f32[2,512,512]{2,1,0:T(8,128)}), f32[2,512,512]{2,1,0:T(8,128)}, u32[]{:S(2)}, u32[]{:S(2)}) %all-to-all-start) | async-done | bytes 2097184 | tf_op jit(solution)/shard_map/all_to_all | solution.py:27
  82.2 1.9 %reduce_sum.18 = f32[512,512]{1,0:T(8,128)S(1)} reduce(f32[2,512,512]{2,1,0:T(8,128)} %all-to-all-done, f32[]{:T(128)} %constant.32.clone.1), dimensions={0}, to_apply=%region_0.1 | reduce | flops 262144 | bytes 3145732 | tf_op jit(solution)/shard_map/reduce_sum | solution.py:28
  84.1 0.3 fusion.35
  84.4 1.0 broadcast_in_dim.5
  85.5 3.6 %all-to-all-start.1 = ((bf16[2,512,512]{2,1,0:T(8,128)(2,1)}), bf16[2,512,512]{2,1,0:T(8,128)(2,1)S(1)}, u32[]{:S(2)}, u32[]{:S(2)}) async-start(bf16[2,512,512]{2,1,0:T(8,128)(2,1)} %broadcast_in_dim.5), calls=%async_computation.1 | async-start | bytes 2097152 | tf_op jit(solution)/shard_map/all_to_all | solution.py:33
  89.1 9.4 %all-to-all-done.1 = bf16[2,512,512]{2,1,0:T(8,128)(2,1)S(1)} async-done(((bf16[2,512,512]{2,1,0:T(8,128)(2,1)}), bf16[2,512,512]{2,1,0:T(8,128)(2,1)S(1)}, u32[]{:S(2)}, u32[]{:S(2)}) %all-to-all-start.1) | async-done | bytes 1048608 | tf_op jit(solution)/shard_map/all_to_all | solution.py:33
  98.4 1.7 fusion.23
  100.1 1.5 fusion.31
  101.7 20.8 %collective-permute-done.4 = f32[256,512]{1,0:T(8,128)S(1)} collective-permute-done((f32[256,512]{1,0:T(8,128)S(1)}, f32[256,512]{1,0:T(8,128)S(1)}, u32[]{:S(2)}, u32[]{:S(2)}) %collective-permute-start.4) | collective-permute-done | bytes 524320 | tf_op jit(solution)/shard_map/ppermute | solution.py:16
  122.5 1.5 fusion.24
  124.0 0.5 fusion.32
  124.4 0.3 collective-permute-start.5
  124.7 1.5 fusion.48
  126.2 11.6 %collective-permute-done.5 = f32[256,512]{1,0:T(8,128)S(1)} collective-permute-done((f32[256,512]{1,0:T(8,128)S(1)}, f32[256,512]{1,0:T(8,128)S(1)}, u32[]{:S(2)}, u32[]{:S(2)}) %collective-permute-start.5) | collective-permute-done | bytes 524320 | tf_op jit(solution)/shard_map/ppermute | solution.py:16
  137.8 1.5 fusion.25
  139.3 0.5 fusion.33
  139.9 0.4 fusion.45
  140.3 0.4 fusion.42
  140.8 12.3 %collective-permute-done.6 = f32[256,512]{1,0:T(8,128)S(1)} collective-permute-done((f32[256,512]{1,0:T(8,128)S(1)}, f32[256,512]{1,0:T(8,128)S(1)}, u32[]{:S(2)}, u32[]{:S(2)}) %collective-permute-start.6) | collective-permute-done | bytes 524320 | tf_op jit(solution)/shard_map/ppermute | solution.py:16
  153.1 1.5 fusion.26
  154.6 1.8 add_multiply_fusion
  156.4 4.8 %all-to-all-start.2 = ((f32[2,512,512]{2,1,0:T(8,128)}), f32[2,512,512]{2,1,0:T(8,128)}, u32[]{:S(2)}, u32[]{:S(2)}) async-start(f32[2,512,512]{2,1,0:T(8,128)} %bitcast.138), calls=%async_computation.2 | async-start | bytes 4194304 | tf_op jit(solution)/shard_map/all_to_all | solution.py:27
  161.3 0.5 fusion.34
  161.8 13.2 %collective-permute-done.7 = f32[256,512]{1,0:T(8,128)S(1)} collective-permute-done((f32[256,512]{1,0:T(8,128)S(1)}, f32[256,512]{1,0:T(8,128)S(1)}, u32[]{:S(2)}, u32[]{:S(2)}) %collective-permute-start.7) | collective-permute-done | bytes 524320 | tf_op jit(solution)/shard_map/ppermute | solution.py:16
  175.1 0.8 copy-done.7
  175.8 5.1 %all-to-all-done.2 = f32[2,512,512]{2,1,0:T(8,128)} async-done(((f32[2,512,512]{2,1,0:T(8,128)}), f32[2,512,512]{2,1,0:T(8,128)}, u32[]{:S(2)}, u32[]{:S(2)}) %all-to-all-start.2) | async-done | bytes 2097184 | tf_op jit(solution)/shard_map/all_to_all | solution.py:27
  181.0 2.9 %reduce_sum.19 = f32[512,512]{1,0:T(8,128)} reduce(f32[2,512,512]{2,1,0:T(8,128)} %all-to-all-done.2, f32[]{:T(128)} %constant.32.clone.1), dimensions={0}, to_apply=%region_1.2 | reduce | flops 262144 | bytes 3145732 | tf_op jit(solution)/shard_map/reduce_sum | solution.py:28
  183.8 2.6 %multiply_add_fusion = f32[512,512]{1,0:T(8,128)} fusion(f32[512,512]{1,0:T(8,128)} %reduce_sum.19, f32[512,512]{1,0:T(8,128)S(1)} %reduce_sum.18, f32[1024,512]{1,0:T(8,128)S(1)} %copy-done.2, s32[]{:T(128)S(6)} %select_n.14), kind=kLoop, calls=%fused_computation.54 | loop fusion | flops 1048576 | bytes 4194308 | tf_op jit(solution)/shard_map/add | solution.py:77
  186.5 0.8 copy.17
  (27 shorter events, 0.6 us)
Async XLA Ops:
  0.6 3.4 %copy-start = (s32[4]{0:T(128)S(1)}, s32[4]{0:T(128)}, u32[]{:S(2)}) copy-start(s32[4]{0:T(128)} %param.7) | copy-start | bytes 52
  0.6 3.2 %copy-start.1 = (f32[1024,512]{1,0:T(8,128)S(1)}, f32[1024,512]{1,0:T(8,128)}, u32[]{:S(2)}) copy-start(f32[1024,512]{1,0:T(8,128)} %param.5) | copy-start | bytes 6291460
  3.9 45.8 %copy-start.3 = (bf16[1024,1,8,256]{3,0,2,1:T(8,128)(2,1)}, bf16[1024,1,8,256]{3,0,2,1:T(8,128)(2,1)S(1)}, u32[]{:S(2)}) copy-start(bf16[1024,1,8,256]{3,0,2,1:T(8,128)(2,1)S(1)} %copy.15) | copy-start | bytes 12582916
  3.9 1.4 copy-start.6
  6.3 15.1 %collective-permute-start = (f32[256,512]{1,0:T(8,128)S(1)}, f32[256,512]{1,0:T(8,128)S(1)}, u32[]{:S(2)}, u32[]{:S(2)}) collective-permute-start(f32[256,512]{1,0:T(8,128)S(1)} %fusion.27), channel_id=1, source_target_pairs={{0,2},{2,4},{4,6},{6,8},{8,10},{10,12},{12,14},{14,16},{16,18},{18... | collective-permute-start | bytes 1572872 | tf_op jit(solution)/shard_map/ppermute | solution.py:16
  22.3 13.2 %collective-permute-start.1 = (f32[256,512]{1,0:T(8,128)S(1)}, f32[256,512]{1,0:T(8,128)S(1)}, u32[]{:S(2)}, u32[]{:S(2)}) collective-permute-start(f32[256,512]{1,0:T(8,128)S(1)} %fusion.28), channel_id=1, source_target_pairs={{0,2},{2,4},{4,6},{6,8},{8,10},{10,12},{12,14},{14,16},{16,18},{18... | collective-permute-start | bytes 1572872 | tf_op jit(solution)/shard_map/ppermute | solution.py:16
  36.5 13.2 %collective-permute-start.2 = (f32[256,512]{1,0:T(8,128)S(1)}, f32[256,512]{1,0:T(8,128)S(1)}, u32[]{:S(2)}, u32[]{:S(2)}) collective-permute-start(f32[256,512]{1,0:T(8,128)S(1)} %fusion.29), channel_id=1, source_target_pairs={{0,2},{2,4},{4,6},{6,8},{8,10},{10,12},{12,14},{14,16},{16,18},{18... | collective-permute-start | bytes 1572872 | tf_op jit(solution)/shard_map/ppermute | solution.py:16
  49.7 2.3 %copy-start.4 = (f32[256,512]{1,0:T(8,128)}, f32[256,512]{1,0:T(8,128)S(1)}, u32[]{:S(2)}) copy-start(f32[256,512]{1,0:T(8,128)S(1)} %collective-permute-done.2) | copy-start | bytes 1572868
  50.2 1.8 copy-start.5
  52.0 30.2 %all-to-all-start = ((f32[2,512,512]{2,1,0:T(8,128)}), f32[2,512,512]{2,1,0:T(8,128)}, u32[]{:S(2)}, u32[]{:S(2)}) async-start(f32[2,512,512]{2,1,0:T(8,128)} %bitcast.137), calls=%async_computation | async-start | bytes 4194304 | tf_op jit(solution)/shard_map/all_to_all | solution.py:27
  59.3 29.8 %collective-permute-start.3 = (f32[256,512]{1,0:T(8,128)}, f32[256,512]{1,0:T(8,128)}, u32[]{:S(2)}, u32[]{:S(2)}) collective-permute-start(f32[256,512]{1,0:T(8,128)} %fusion.30), channel_id=1, source_target_pairs={{0,2},{2,4},{4,6},{6,8},{8,10},{10,12},{12,14},{14,16},{16,18},{18... | collective-permute-start | bytes 1572872 | tf_op jit(solution)/shard_map/ppermute | solution.py:16
  85.5 13.0 %all-to-all-start.1 = ((bf16[2,512,512]{2,1,0:T(8,128)(2,1)}), bf16[2,512,512]{2,1,0:T(8,128)(2,1)S(1)}, u32[]{:S(2)}, u32[]{:S(2)}) async-start(bf16[2,512,512]{2,1,0:T(8,128)(2,1)} %broadcast_in_dim.5), calls=%async_computation.1 | async-start | bytes 2097152 | tf_op jit(solution)/shard_map/all_to_all | solution.py:33
  101.6 20.8 %collective-permute-start.4 = (f32[256,512]{1,0:T(8,128)S(1)}, f32[256,512]{1,0:T(8,128)S(1)}, u32[]{:S(2)}, u32[]{:S(2)}) collective-permute-start(f32[256,512]{1,0:T(8,128)S(1)} %fusion.31), channel_id=1, source_target_pairs={{0,2},{2,4},{4,6},{6,8},{8,10},{10,12},{12,14},{14,16},{16,18},{18... | collective-permute-start | bytes 1572872 | tf_op jit(solution)/shard_map/ppermute | solution.py:16
  124.4 13.4 %collective-permute-start.5 = (f32[256,512]{1,0:T(8,128)S(1)}, f32[256,512]{1,0:T(8,128)S(1)}, u32[]{:S(2)}, u32[]{:S(2)}) collective-permute-start(f32[256,512]{1,0:T(8,128)S(1)} %fusion.32), channel_id=1, source_target_pairs={{0,2},{2,4},{4,6},{6,8},{8,10},{10,12},{12,14},{14,16},{16,18},{18... | collective-permute-start | bytes 1572872 | tf_op jit(solution)/shard_map/ppermute | solution.py:16
  139.8 13.3 %collective-permute-start.6 = (f32[256,512]{1,0:T(8,128)S(1)}, f32[256,512]{1,0:T(8,128)S(1)}, u32[]{:S(2)}, u32[]{:S(2)}) collective-permute-start(f32[256,512]{1,0:T(8,128)S(1)} %fusion.33), channel_id=1, source_target_pairs={{0,2},{2,4},{4,6},{6,8},{8,10},{10,12},{12,14},{14,16},{16,18},{18... | collective-permute-start | bytes 1572872 | tf_op jit(solution)/shard_map/ppermute | solution.py:16
  156.4 24.5 %all-to-all-start.2 = ((f32[2,512,512]{2,1,0:T(8,128)}), f32[2,512,512]{2,1,0:T(8,128)}, u32[]{:S(2)}, u32[]{:S(2)}) async-start(f32[2,512,512]{2,1,0:T(8,128)} %bitcast.138), calls=%async_computation.2 | async-start | bytes 4194304 | tf_op jit(solution)/shard_map/all_to_all | solution.py:27
  161.7 22.1 %copy-start.2 = (f32[1024,512]{1,0:T(8,128)S(1)}, f32[1024,512]{1,0:T(8,128)}, u32[]{:S(2)}) copy-start(f32[1024,512]{1,0:T(8,128)} %param.5) | copy-start | bytes 6291460
  161.8 13.3 %collective-permute-start.7 = (f32[256,512]{1,0:T(8,128)S(1)}, f32[256,512]{1,0:T(8,128)S(1)}, u32[]{:S(2)}, u32[]{:S(2)}) collective-permute-start(f32[256,512]{1,0:T(8,128)S(1)} %fusion.34), channel_id=1, source_target_pairs={{0,2},{2,4},{4,6},{6,8},{8,10},{10,12},{12,14},{14,16},{16,18},{18... | collective-permute-start | bytes 1572872 | tf_op jit(solution)/shard_map/ppermute | solution.py:16
  175.0 0.8 copy-start.7
  183.8 2.6 %copy-start.8 = (f32[256,512]{1,0:T(8,128)S(1)}, f32[256,512]{1,0:T(8,128)}, u32[]{:S(2)}) copy-start(f32[256,512]{1,0:T(8,128)} %copy-done.7) | copy-start | bytes 1572868
where the time goes:
time: 188 us; the launch traced here: 187 us
  waiting for transfers between devices  135 us (72%)
  matrix products  22.1 us (12%)
  starting transfers between devices  14 us (7%)
  other arithmetic  7.84 us (4%)
  local copies, waits for them, and re-layouts  7.12 us (4%)
    ppermute x8, waiting for transfers between devices, shifted(): lax.ppermute(array, axis, [(i, (i + by) % count) for i in range(count)])  97.9 us
    all_to_all x2, waiting for transfers between devices, summed_on_arrival(): lax.all_to_all(parts, axis, split_axis=0, concat_axis=0, tiled=True)  28 us
    all_to_all x2, starting transfers between devices, summed_on_arrival(): lax.all_to_all(parts, axis, split_axis=0, concat_axis=0, tiled=True)  9.63 us
    all_to_all x1, waiting for transfers between devices, from_everyone(): return lax.all_to_all(copies, axis, split_axis=0, concat_axis=0, tiled=True)  9.36 us
    dot_general x8, matrix products, per_device(): lax.dot_general(loads_bf, block_bf, (((1,), (1,)), ((), ())), preferred_e...  8.1 us
    dot_general x8, matrix products, per_device(): jnp.dot(resid, block_bf, preferred_element_type=jnp.float32) * scale  7.31 us
    dot_general x8, matrix products, per_device(): lax.dot_general(resid, loads_bf, (((0,), (0,)), ((), ())), preferred_elem...  6.7 us
    unnamed x22, local copies, waits for them, and re-layouts  6.08 us
  transfers between devices with their start and end apart: 11, of which 10 were waited for; matrix products, arithmetic and copies ran while one was open for 5% of the time, Pallas kernels for 0%

commit v1 on v0

v1 whole, which is shorter than its diff:
```python
import jax
import jax.numpy as jnp
from jax import lax
from jax.experimental import pallas as pl
from jax.experimental.pallas import tpu as pltpu
from jax.sharding import PartitionSpec as P

RUN_LEN = 256
STEPS = 8

map_rate = 0.1
load_rate = 0.05

SPAN = 240.0
TOP_ROWS = 16
TINY = 1e-30

VMEM = pl.BlockSpec(memory_space=pltpu.VMEM)
SMEM = pl.BlockSpec(memory_space=pltpu.SMEM)
f32 = jnp.float32
bf16 = jnp.bfloat16


def local_call(body, small, arrays, outs, *, name, aliases=None, temp_mib=12):
    arrays = [pltpu.with_memory_space_constraint(x, pltpu.VMEM) for x in arrays]
    result = pl.pallas_call(
        body,
        in_specs=[SMEM] * len(small) + [VMEM] * len(arrays),
        out_specs=[VMEM] * len(outs),
        out_shape=[pltpu.VMEM(shape, dtype) for shape, dtype in outs],
        input_output_aliases=aliases or {},
        compiler_params=pltpu.CompilerParams(vmem_limit_bytes=temp_mib * 2**20),
        name=name,
    )(*small, *arrays)
    return result


def encode(block, out_ref):
    rank = block.shape[0]
    size = jnp.abs(block)
    top = jnp.max(size, axis=0, keepdims=True)
    top = jnp.maximum(top * (1.0 + 2.0**-6), TINY).astype(bf16)
    wide = top.astype(f32)
    code = jnp.exp2(size * (SPAN / wide) - SPAN / 2)
    out_ref[0:rank, :] = jnp.where(block < 0, -code, code).astype(bf16)
    out_ref[rank : rank + TOP_ROWS, :] = jnp.broadcast_to(top, (TOP_ROWS, block.shape[1]))


def decode(in_ref):
    rank = in_ref.shape[0] - TOP_ROWS
    code = in_ref[0:rank, :].astype(f32)
    top = in_ref[rank : rank + 1, :].astype(f32)
    size = (jnp.log2(jnp.abs(code)) + SPAN / 2) * (top / SPAN)
    return jnp.where(code < 0, -size, size)


def add_pending(acc_ref, pending, fresh):
    first = fresh
    for resid_ref, block_ref in pending:
        part = lax.dot_general(
            resid_ref[...], block_ref[...], (((1,), (1,)), ((), ())), preferred_element_type=f32
        )
        acc_ref[...] = part if first else acc_ref[...] + part
        first = False


def step_call(core, counts, block, tile, loads, loads_t, acc, pending, *, active, fresh, coded, name):
    frames, rank = loads.shape
    width = tile.shape[1]
    scale = 1.0 / rank**0.5
    n_pend = len(pending)
    has_acc = acc is not None

    def body(*refs):
        core_ref, counts_ref, block_ref, tile_ref, loads_ref, loads_t_ref = refs[:6]
        at = 6
        pend = [(refs[at + 2 * i], refs[at + 2 * i + 1]) for i in range(n_pend)]
        at += 2 * n_pend + (1 if has_acc else 0)
        out_ref, resid_ref, bb_ref, acc_ref = refs[at : at + 4]

        @pl.when(core_ref[0] == active)
        def _():
            held = decode(block_ref) if coded else block_ref[...]
            bb = held.astype(bf16)
            bb_ref[...] = bb
            rows = lax.broadcasted_iota(jnp.int32, (RUN_LEN, width), 0)
            for run in range(frames // RUN_LEN):
                at = slice(run * RUN_LEN, (run + 1) * RUN_LEN)
                prod = jnp.dot(loads_ref[at, :], bb, preferred_element_type=f32)
                diff = tile_ref[at, :].astype(f32) - prod * scale
                resid_ref[at, :] = jnp.where(rows < counts_ref[run], diff, 0.0).astype(bf16)
            grad = jnp.dot(loads_t_ref[...], resid_ref[...], preferred_element_type=f32)
            encode(held + (map_rate * scale) * grad, out_ref)

        if n_pend:

            @pl.when(core_ref[0] != active)
            def _():
                add_pending(acc_ref, pend, fresh)

    flat = [x for pair in pending for x in pair]
    arrays = [block, tile, loads, loads_t, *flat] + ([acc] if has_acc else [])
    outs = [
        ((rank + TOP_ROWS, width), bf16),
        ((frames, width), bf16),
        ((rank, width), bf16),
        ((frames, rank), f32),
    ]
    aliases = {len(arrays) + 1: 3} if has_acc else {}
    return local_call(body, [core, counts], arrays, outs, name=name, aliases=aliases)


def gather_call(core, acc, pending, start, rows, *, active, name):
    frames, rank = acc.shape

    def body(core_ref, start_ref, resid_ref, bb_ref, acc_in_ref, out_ref, acc_ref):
        @pl.when(core_ref[0] == active)
        def _():
            add_pending(acc_ref, [(resid_ref, bb_ref)], False)

        if rows == frames:
            out_ref[...] = acc_ref[...].astype(bf16)
        else:
            first = pl.multiple_of(start_ref[0] * rows, rows)
            out_ref[...] = acc_ref[pl.ds(first, rows), :].astype(bf16)

    outs = [((rows, rank), bf16), ((frames, rank), f32)]
    return local_call(body, [core, start], [*pending, acc], outs, name=name, aliases={4: 1})


def update_call(loadings, acc, arrived, *, name):
    frames, rank = acc.shape
    factor = load_rate / rank**0.5

    def body(loadings_ref, acc_ref, arrived_ref, loads_ref, loads_t_ref):
        for at in range(0, frames, RUN_LEN):
            rows = slice(at, at + RUN_LEN)
            new = loadings_ref[rows, :] + factor * (acc_ref[rows, :] + arrived_ref[rows, :].astype(f32))
            new = new.astype(bf16)
            loads_ref[rows, :] = new
            loads_t_ref[:, rows] = new.T

    outs = [((frames, rank), bf16), ((rank, frames), bf16)]
    return local_call(body, [], [loadings, acc, arrived], outs, name=name)


def first_call(loadings, maps, *, name):
    frames, rank = loadings.shape

    def body(loadings_ref, maps_ref, loads_ref, loads_t_ref, block_ref):
        for at in range(0, frames, RUN_LEN):
            rows = slice(at, at + RUN_LEN)
            new = loadings_ref[rows, :].astype(bf16)
            loads_ref[rows, :] = new
            loads_t_ref[:, rows] = new.T
        block_ref[...] = maps_ref[...].T

    outs = [((frames, rank), bf16), ((rank, frames), bf16), ((rank, maps.shape[0]), f32)]
    return local_call(body, [], [loadings, maps], outs, name=name)


def final_call(panel, loadings, acc, arrived, *, name):
    rows, rank = arrived.shape
    factor = load_rate / rank**0.5

    def body(panel_ref, loadings_ref, acc_ref, arrived_ref, out_ref):
        own = pl.ds(pl.multiple_of(panel_ref[0] * rows, rows), rows)
        out_ref[...] = loadings_ref[own, :] + factor * (
            acc_ref[own, :] + arrived_ref[...].astype(f32)
        )

    return local_call(body, [panel], [loadings, acc, arrived], [((rows, rank), f32)], name=name)[0]


def maps_call(core, block_a, block_b, *, name):
    rank = block_a.shape[0] - TOP_ROWS
    width = block_a.shape[1]

    def body(core_ref, a_ref, b_ref, out_ref):
        @pl.when(core_ref[0] == 0)
        def _():
            out_ref[...] = decode(a_ref).T

        @pl.when(core_ref[0] == 1)
        def _():
            out_ref[...] = decode(b_ref).T

    return local_call(body, [core], [block_a, block_b], [((width, rank), f32)], name=name)[0]


def per_device(tiles, loadings, maps, run_counts):
    frames, rank = loadings.shape
    n_blk = lax.axis_size("blk")
    n_panel = lax.axis_size("panel")
    core = (lax.axis_index("blk") % 2).astype(jnp.int32).reshape(1)
    panel = lax.axis_index("panel").astype(jnp.int32).reshape(1)
    other = n_panel - 1 - panel

    def hop(payload, from_core):
        pairs = [(i, (i + 1) % n_blk) for i in range(n_blk) if i % 2 == from_core]
        return lax.ppermute(payload, "blk", pairs)

    def swap(payload):
        return lax.ppermute(payload, "panel", [(i, n_panel - 1 - i) for i in range(n_panel)])

    tile = [tiles[:, 0, s, :] for s in range(STEPS)]
    loads, loads_t, block = first_call(loadings, maps[0, 0], name="first")
    chain = [block, block]
    acc = None
    half = STEPS // 2
    last = [None, None]
    for step in range(STEPS):
        for which in range(2):
            active = (step + which) % 2
            pending = []
            if which == 1:
                pending = ([] if step % half == 0 else [last[1]]) + [last[0]]
            payload, resid, bb, acc = step_call(
                core,
                run_counts,
                chain[which],
                tile[step],
                loads,
                loads_t,
                acc,
                pending,
                active=active,
                fresh=step < 2,
                coded=step > 0,
                name=f"step{step}{'EO'[which]}",
            )
            last[which] = (resid, bb)
            with jax.named_scope(f"hop{step}{'EO'[which]}"):
                chain[which] = hop(payload, active)
        if step == half - 1:
            mine, acc = gather_call(
                core, acc, last[1], other, frames, active=0, name="gather_mid"
            )
            with jax.named_scope("swap_mid"):
                arrived = swap(mine)
            loads, loads_t = update_call(loadings, acc, arrived, name="update")
    mine, acc = gather_call(
        core, acc, last[1], other, frames // n_panel, active=0, name="gather_end"
    )
    with jax.named_scope("swap_end"):
        arrived = swap(mine)
    maps_after = maps_call(core, chain[0], chain[1], name="maps_after")
    loadings_out = final_call(panel, loadings, acc, arrived, name="loadings_out")
    return loadings_out, maps_after.reshape(maps.shape)


def solution(mesh):
    in_specs = (
        P("blk", "panel", None, None),
        P("blk", None),
        P("blk", "panel", None, None),
        P("blk"),
    )
    out_specs = (P(("blk", "panel"), None), P("blk", "panel", None, None))
    return jax.shard_map(
        per_device, mesh=mesh, in_specs=in_specs, out_specs=out_specs, check_vma=False
    )
```

time: 188 us -> 149 us (0.79)
  the two profiles are of different devices: /device:TPU:6 before, /device:TPU:8 now
where the time goes in v1:
time: 149 us
  waiting for transfers between devices  68.1 us (46%)
  local copies, waits for them, and re-layouts  29.7 us (20%)
  Pallas kernels  25.1 us (17%)
  starting transfers between devices  24.6 us (17%)
    ppermute x16, waiting for transfers between devices, hop(): return lax.ppermute(payload, 'blk', pairs)  55.6 us
    pallas_call x22, Pallas kernels, local_call(): pl.pallas_call(body, in_specs=[SMEM] * len(small) + [VMEM] * len(arrays),...  25.1 us
    slice x1, local copies, waits for them, and re-layouts, per_device(): tile = [tiles[:, 0, s, :] for s in range(STEPS)]  22.3 us
    ppermute x16, starting transfers between devices, hop(): return lax.ppermute(payload, 'blk', pairs)  21.4 us
    ppermute x2, waiting for transfers between devices, swap(): lax.ppermute(payload, 'panel', [(i, n_panel - 1 - i) for i in range(n_pan...  12.5 us
    unnamed x44, local copies, waits for them, and re-layouts  7.34 us
    ppermute x2, starting transfers between devices, swap(): lax.ppermute(payload, 'panel', [(i, n_panel - 1 - i) for i in range(n_pan...  3.13 us
  transfers between devices with their start and end apart: 18, of which 7 were waited for; matrix products, arithmetic and copies ran while one was open for 2% of the time, Pallas kernels for 12%

profile of v1, /device:TPU:8, one launch (start us, length us, event | category | flops | bytes accessed | tf_op | source)
XLA Modules:
  0.0 148.6 jit_solution(2445438436736255883)
XLA Ops:
  0.6 22.3 %fusion = (bf16[1024,1,1,256]{3,2,1,0:T(2,128)(2,1)}, bf16[1024,1,1,256]{3,2,1,0:T(2,128)(2,1)}, bf16[1024,1,1,256]{3,2,1,0:T(2,128)(2,1)}, bf16[1024,1,1,256]{3...) fusion(bf16[1024,1,8,256]{3,2,1,0:T(8,128)(2,1)} %param.4), kind=kLoop, calls=%fused_computation.8 | loop fusion | bytes 8388608 | tf_op jit(solution)/shard_map/slice | solution.py:206
  23.0 0.9 copy.54
  23.9 1.1 copy-done.5
  25.6 1.6 %step0E.1 = (bf16[528,256]{1,0:T(8,128)(2,1)S(1)}, bf16[1024,256]{1,0:T(8,128)(2,1)S(1)}, bf16[512,256]{1,0:T(8,128)(2,1)S(1)}, f32[1024,512]{1,0:T(8,128)S(1)}) custom-call(s32[1]{0:T(128)} %bitcast.1.refs_0_.core_ref, s32[4]{0:T(128)S(1)} %copy-done.10, f32[512,256]{1,0:T(8,128)S(1)} %get-tuple-element.75.refs_2_, bf16[1024,256]{1,0:T(8,128)(2,1)S(1)} %bitcast.29, ...), custom_call_target="tpu_custom_call" | custom-call | tf_op jit(solution)/shard_map/step0E/pallas_call | solution.py:26
  27.2 1.3 collective-permute-start.1
  28.5 1.0 step0O.1
  29.5 1.3 collective-permute-start
  30.9 0.5 step1E.1
  31.5 1.3 collective-permute-start.3
  32.8 10.9 %collective-permute-done.refs_2_ = bf16[528,256]{1,0:T(8,128)(2,1)S(1)} collective-permute-done((bf16[528,256]{1,0:T(8,128)(2,1)S(1)}, bf16[528,256]{1,0:T(8,128)(2,1)S(1)}, u32[]{:S(2)}, u32[]{:S(2)}) %collective-permute-start) | collective-permute-done | bytes 270368 | tf_op jit(solution)/shard_map/hop0O/ppermute | solution.py:201
  43.7 1.7 %step1O.1 = (bf16[528,256]{1,0:T(8,128)(2,1)S(1)}, bf16[1024,256]{1,0:T(8,128)(2,1)S(1)}, bf16[512,256]{1,0:T(8,128)(2,1)S(1)}, f32[1024,512]{1,0:T(8,128)S(1)}) custom-call(s32[1]{0:T(128)} %bitcast.1.refs_0_.core_ref, s32[4]{0:T(128)S(1)} %copy-done.10, bf16[528,256]{1,0:T(8,128)(2,1)S(1)} %collective-permute-done.refs_2_, ...), custom_call_target="tpu_custom_call", output_to_operand_aliasing={{3}: (10, {})} | custom-call | tf_op jit(solution)/shard_map/step1O/pallas_call | solution.py:26
  45.4 1.3 collective-permute-start.2
  46.9 2.4 %step2E.1 = (bf16[528,256]{1,0:T(8,128)(2,1)}, bf16[1024,256]{1,0:T(8,128)(2,1)S(1)}, bf16[512,256]{1,0:T(8,128)(2,1)S(1)}, f32[1024,512]{1,0:T(8,128)S(1)}) custom-call(s32[1]{0:T(128)} %bitcast.1.refs_0_.core_ref, s32[4]{0:T(128)S(1)} %copy-done.10, bf16[528,256]{1,0:T(8,128)(2,1)S(1)} %collective-permute-done.3.refs_2_, ...), custom_call_target="tpu_custom_call", output_to_operand_aliasing={{3}: (6, {})} | custom-call | tf_op jit(solution)/shard_map/step2E/pallas_call | solution.py:26
  49.3 2.0 %collective-permute-start.5 = (bf16[528,256]{1,0:T(8,128)(2,1)}, bf16[528,256]{1,0:T(8,128)(2,1)}, u32[]{:S(2)}, u32[]{:S(2)}) collective-permute-start(bf16[528,256]{1,0:T(8,128)(2,1)} %get-tuple-element.100), channel_id=1, source_target_pairs={{0,2},{4,6},{8,10},{12,14},{16,18},{20,22},{24,26},{28,30},{32,34}... | collective-permute-start | bytes 811016 | tf_op jit(solution)/shard_map/hop2E/ppermute | solution.py:201
  51.3 2.0 %step2O.1 = (bf16[528,256]{1,0:T(8,128)(2,1)}, bf16[1024,256]{1,0:T(8,128)(2,1)S(1)}, bf16[512,256]{1,0:T(8,128)(2,1)S(1)}, f32[1024,512]{1,0:T(8,128)S(1)}) custom-call(s32[1]{0:T(128)} %bitcast.1.refs_0_.core_ref, s32[4]{0:T(128)S(1)} %copy-done.10, bf16[528,256]{1,0:T(8,128)(2,1)S(1)} %collective-permute-done.2.refs_2_, ...), custom_call_target="tpu_custom_call", output_to_operand_aliasing={{3}: (10, {})} | custom-call | tf_op jit(solution)/shard_map/step2O/pallas_call | solution.py:26
  53.2 0.8 copy-done.6
  54.0 0.7 copy-done.8
  54.7 1.3 collective-permute-start.4
  56.0 1.4 copy.51
  57.6 1.2 step3E.1
  58.8 9.7 %collective-permute-done.4.refs_2_ = bf16[528,256]{1,0:T(8,128)(2,1)S(1)} collective-permute-done((bf16[528,256]{1,0:T(8,128)(2,1)}, bf16[528,256]{1,0:T(8,128)(2,1)S(1)}, u32[]{:S(2)}, u32[]{:S(2)}) %collective-permute-start.4) | collective-permute-done | bytes 270368 | tf_op jit(solution)/shard_map/hop2O/ppermute | solution.py:201
  68.5 1.7 %step3O.1 = (bf16[528,256]{1,0:T(8,128)(2,1)S(1)}, bf16[1024,256]{1,0:T(8,128)(2,1)S(1)}, bf16[512,256]{1,0:T(8,128)(2,1)S(1)}, f32[1024,512]{1,0:T(8,128)S(1)}) custom-call(s32[1]{0:T(128)} %bitcast.1.refs_0_.core_ref, s32[4]{0:T(128)S(1)} %copy-done.10, bf16[528,256]{1,0:T(8,128)(2,1)S(1)} %collective-permute-done.4.refs_2_, ...), custom_call_target="tpu_custom_call", output_to_operand_aliasing={{3}: (10, {})} | custom-call | tf_op jit(solution)/shard_map/step3O/pallas_call | solution.py:26
  70.3 0.6 gather_mid.1
  70.9 1.6 %collective-permute-start.7 = (bf16[1024,512]{1,0:T(8,128)(2,1)S(1)}, bf16[1024,512]{1,0:T(8,128)(2,1)S(1)}, u32[]{:S(2)}, u32[]{:S(2)}) collective-permute-start(bf16[1024,512]{1,0:T(8,128)(2,1)S(1)} %get-tuple-element.110), channel_id=1, source_target_pairs={{0,1},{1,0},{2,3},{3,2},{4,5},{5,4},{6,7},{7,6},{8,9},{9,8},{10,11... | collective-permute-start | bytes 3145736 | tf_op jit(solution)/shard_map/swap_mid/ppermute | solution.py:204
  72.4 1.3 collective-permute-start.8
  73.7 1.3 collective-permute-start.6
  75.1 12.5 %collective-permute-done.7.arrived_ref = bf16[1024,512]{1,0:T(8,128)(2,1)S(1)} collective-permute-done((bf16[1024,512]{1,0:T(8,128)(2,1)S(1)}, bf16[1024,512]{1,0:T(8,128)(2,1)S(1)}, u32[]{:S(2)}, u32[]{:S(2)}) %collective-permute-start.7) | collective-permute-done | bytes 1048608 | tf_op jit(solution)/shard_map/swap_mid/ppermute | solution.py:204
  88.1 1.7 %step4E.1 = (bf16[528,256]{1,0:T(8,128)(2,1)S(1)}, bf16[1024,256]{1,0:T(8,128)(2,1)S(1)}, bf16[512,256]{1,0:T(8,128)(2,1)S(1)}, f32[1024,512]{1,0:T(8,128)S(1)}) custom-call(s32[1]{0:T(128)} %bitcast.1.refs_0_.core_ref, s32[4]{0:T(128)S(1)} %copy-done.10, bf16[528,256]{1,0:T(8,128)(2,1)S(1)} %collective-permute-done.8.refs_2_, ...), custom_call_target="tpu_custom_call", output_to_operand_aliasing={{3}: (6, {})} | custom-call | tf_op jit(solution)/shard_map/step4E/pallas_call | solution.py:26
  89.8 1.3 collective-permute-start.10
  91.1 1.0 step4O.1
  92.1 1.3 collective-permute-start.9
  94.1 1.3 collective-permute-start.12
  95.4 10.2 %collective-permute-done.9.refs_2_ = bf16[528,256]{1,0:T(8,128)(2,1)S(1)} collective-permute-done((bf16[528,256]{1,0:T(8,128)(2,1)S(1)}, bf16[528,256]{1,0:T(8,128)(2,1)S(1)}, u32[]{:S(2)}, u32[]{:S(2)}) %collective-permute-start.9) | collective-permute-done | bytes 270368 | tf_op jit(solution)/shard_map/hop4O/ppermute | solution.py:201
  105.6 1.7 %step5O.1 = (bf16[528,256]{1,0:T(8,128)(2,1)S(1)}, bf16[1024,256]{1,0:T(8,128)(2,1)S(1)}, bf16[512,256]{1,0:T(8,128)(2,1)S(1)}, f32[1024,512]{1,0:T(8,128)S(1)}) custom-call(s32[1]{0:T(128)} %bitcast.1.refs_0_.core_ref, s32[4]{0:T(128)S(1)} %copy-done.10, bf16[528,256]{1,0:T(8,128)(2,1)S(1)} %collective-permute-done.9.refs_2_, ...), custom_call_target="tpu_custom_call", output_to_operand_aliasing={{3}: (10, {})} | custom-call | tf_op jit(solution)/shard_map/step5O/pallas_call | solution.py:26
  107.4 1.3 collective-permute-start.11
  108.8 0.9 collective-permute-done.12.refs_2_
  109.7 1.7 %step6E.1 = (bf16[528,256]{1,0:T(8,128)(2,1)S(1)}, bf16[1024,256]{1,0:T(8,128)(2,1)S(1)}, bf16[512,256]{1,0:T(8,128)(2,1)S(1)}, f32[1024,512]{1,0:T(8,128)S(1)}) custom-call(s32[1]{0:T(128)} %bitcast.1.refs_0_.core_ref, s32[4]{0:T(128)S(1)} %copy-done.10, bf16[528,256]{1,0:T(8,128)(2,1)S(1)} %collective-permute-done.12.refs_2_, ...), custom_call_target="tpu_custom_call", output_to_operand_aliasing={{3}: (6, {})} | custom-call | tf_op jit(solution)/shard_map/step6E/pallas_call | solution.py:26
  111.4 1.3 collective-permute-start.14
  112.7 1.5 %step6O.1 = (bf16[528,256]{1,0:T(8,128)(2,1)S(1)}, bf16[1024,256]{1,0:T(8,128)(2,1)S(1)}, bf16[512,256]{1,0:T(8,128)(2,1)S(1)}, f32[1024,512]{1,0:T(8,128)S(1)}) custom-call(s32[1]{0:T(128)} %bitcast.1.refs_0_.core_ref, s32[4]{0:T(128)S(1)} %copy-done.10, bf16[528,256]{1,0:T(8,128)(2,1)S(1)} %collective-permute-done.11.refs_2_, ...), custom_call_target="tpu_custom_call", output_to_operand_aliasing={{3}: (10, {})} | custom-call | tf_op jit(solution)/shard_map/step6O/pallas_call | solution.py:26
  114.2 1.3 collective-permute-start.13
  116.2 11.6 %collective-permute-done.13.refs_2_ = bf16[528,256]{1,0:T(8,128)(2,1)S(1)} collective-permute-done((bf16[528,256]{1,0:T(8,128)(2,1)S(1)}, bf16[528,256]{1,0:T(8,128)(2,1)S(1)}, u32[]{:S(2)}, u32[]{:S(2)}) %collective-permute-start.13) | collective-permute-done | bytes 270368 | tf_op jit(solution)/shard_map/hop6O/ppermute | solution.py:201
  127.8 1.7 %step7O.1 = (bf16[528,256]{1,0:T(8,128)(2,1)S(1)}, bf16[1024,256]{1,0:T(8,128)(2,1)S(1)}, bf16[512,256]{1,0:T(8,128)(2,1)S(1)}, f32[1024,512]{1,0:T(8,128)S(1)}) custom-call(s32[1]{0:T(128)} %bitcast.1.refs_0_.core_ref, s32[4]{0:T(128)S(1)} %copy-done.10, bf16[528,256]{1,0:T(8,128)(2,1)S(1)} %collective-permute-done.13.refs_2_, ...), custom_call_target="tpu_custom_call", output_to_operand_aliasing={{3}: (10, {})} | custom-call | tf_op jit(solution)/shard_map/step7O/pallas_call | solution.py:26
  130.1 1.6 %collective-permute-start.15 = (bf16[512,512]{1,0:T(8,128)(2,1)S(1)}, bf16[512,512]{1,0:T(8,128)(2,1)S(1)}, u32[]{:S(2)}, u32[]{:S(2)}) collective-permute-start(bf16[512,512]{1,0:T(8,128)(2,1)S(1)} %get-tuple-element.145), channel_id=1, source_target_pairs={{0,1},{1,0},{2,3},{3,2},{4,5},{5,4},{6,7},{7,6},{8,9},{9,8},{10,11... | collective-permute-start | bytes 1572872 | tf_op jit(solution)/shard_map/swap_end/ppermute | solution.py:204
  131.6 1.3 collective-permute-start.17
  132.9 1.3 collective-permute-start.16
  134.2 12.2 %collective-permute-done.16.a_ref = bf16[528,256]{1,0:T(8,128)(2,1)S(1)} collective-permute-done((bf16[528,256]{1,0:T(8,128)(2,1)S(1)}, bf16[528,256]{1,0:T(8,128)(2,1)S(1)}, u32[]{:S(2)}, u32[]{:S(2)}) %collective-permute-start.16) | collective-permute-done | bytes 270368 | tf_op jit(solution)/shard_map/hop7E/ppermute | solution.py:201
  146.7 0.8 copy.73
  147.6 1.0 copy.72
  (55 shorter events, 3.8 us)
Async XLA Ops:
  0.6 23.2 %copy-start.2 = (f32[1024,512]{1,0:T(8,128)S(1)}, f32[1024,512]{1,0:T(8,128)}, u32[]{:S(2)}) copy-start(f32[1024,512]{1,0:T(8,128)} %loadings_ref.5) | copy-start | bytes 6291460
  23.0 2.5 %copy-start.10 = (s32[4]{0:T(128)S(1)}, s32[4]{0:T(128)}, u32[]{:S(2)}) copy-start(s32[4]{0:T(128)} %refs_1_.31) | copy-start | bytes 52
  23.9 1.7 %copy-start.4 = (bf16[1024,1,1,256]{3,0,2,1:T(8,128)(2,1)S(1)}, bf16[1024,1,1,256]{3,0,2,1:T(8,128)(2,1)}, u32[]{:S(2)}) copy-start(bf16[1024,1,1,256]{3,0,2,1:T(8,128)(2,1)} %copy.54) | copy-start | bytes 1572868
  23.9 1.1 copy-start.5
  25.5 25.7 %copy-start = (bf16[512,1024]{1,0:T(8,128)(2,1)}, bf16[512,1024]{1,0:T(8,128)(2,1)S(1)}, u32[]{:S(2)}) copy-start(bf16[512,1024]{1,0:T(8,128)(2,1)S(1)} %get-tuple-element.77.refs_5_) | copy-start | bytes 3145732
  27.2 3.8 %collective-permute-start.1 = (bf16[528,256]{1,0:T(8,128)(2,1)S(1)}, bf16[528,256]{1,0:T(8,128)(2,1)S(1)}, u32[]{:S(2)}, u32[]{:S(2)}) collective-permute-start(bf16[528,256]{1,0:T(8,128)(2,1)S(1)} %get-tuple-element.84), channel_id=1, source_target_pairs={{0,2},{4,6},{8,10},{12,14},{16,18},{20,22},{24,26},{28,30},{32,34}... | collective-permute-start | bytes 811016 | tf_op jit(solution)/shard_map/hop0E/ppermute | solution.py:201
  28.5 2.3 %copy-start.16 = (bf16[1024,1,1,256]{3,2,1,0:T(2,128)(2,1)S(1)}, bf16[1024,1,1,256]{3,2,1,0:T(2,128)(2,1)}, u32[]{:S(2)}) copy-start(bf16[1024,1,1,256]{3,2,1,0:T(2,128)(2,1)} %get-tuple-element.154) | copy-start | bytes 1572868
  29.5 14.2 %collective-permute-start = (bf16[528,256]{1,0:T(8,128)(2,1)S(1)}, bf16[528,256]{1,0:T(8,128)(2,1)S(1)}, u32[]{:S(2)}, u32[]{:S(2)}) collective-permute-start(bf16[528,256]{1,0:T(8,128)(2,1)S(1)} %get-tuple-element.81), channel_id=1, source_target_pairs={{2,4},{6,8},{10,12},{14,16},{18,20},{22,24},{26,28},{30,32},{34,36... | collective-permute-start | bytes 811016 | tf_op jit(solution)/shard_map/hop0O/ppermute | solution.py:201
  31.5 15.4 %collective-permute-start.3 = (bf16[528,256]{1,0:T(8,128)(2,1)S(1)}, bf16[528,256]{1,0:T(8,128)(2,1)S(1)}, u32[]{:S(2)}, u32[]{:S(2)}) collective-permute-start(bf16[528,256]{1,0:T(8,128)(2,1)S(1)} %get-tuple-element.92), channel_id=1, source_target_pairs={{2,4},{6,8},{10,12},{14,16},{18,20},{22,24},{26,28},{30,32},{34,36... | collective-permute-start | bytes 811016 | tf_op jit(solution)/shard_map/hop1E/ppermute | solution.py:201
  43.7 3.0 %copy-start.15 = (bf16[1024,1,1,256]{3,2,1,0:T(2,128)(2,1)S(1)}, bf16[1024,1,1,256]{3,2,1,0:T(2,128)(2,1)}, u32[]{:S(2)}) copy-start(bf16[1024,1,1,256]{3,2,1,0:T(2,128)(2,1)} %get-tuple-element.153) | copy-start | bytes 1572868
  45.4 5.8 %collective-permute-start.2 = (bf16[528,256]{1,0:T(8,128)(2,1)S(1)}, bf16[528,256]{1,0:T(8,128)(2,1)S(1)}, u32[]{:S(2)}, u32[]{:S(2)}) collective-permute-start(bf16[528,256]{1,0:T(8,128)(2,1)S(1)} %get-tuple-element.89), channel_id=1, source_target_pairs={{0,2},{4,6},{8,10},{12,14},{16,18},{20,22},{24,26},{28,30},{32,34}... | collective-permute-start | bytes 811016 | tf_op jit(solution)/shard_map/hop1O/ppermute | solution.py:201
  49.3 8.2 %collective-permute-start.5 = (bf16[528,256]{1,0:T(8,128)(2,1)}, bf16[528,256]{1,0:T(8,128)(2,1)}, u32[]{:S(2)}, u32[]{:S(2)}) collective-permute-start(bf16[528,256]{1,0:T(8,128)(2,1)} %get-tuple-element.100), channel_id=1, source_target_pairs={{0,2},{4,6},{8,10},{12,14},{16,18},{20,22},{24,26},{28,30},{32,34}... | collective-permute-start | bytes 811016 | tf_op jit(solution)/shard_map/hop2E/ppermute | solution.py:201
  53.2 0.8 copy-start.6
  54.0 0.7 copy-start.8
  54.7 13.8 %collective-permute-start.4 = (bf16[528,256]{1,0:T(8,128)(2,1)}, bf16[528,256]{1,0:T(8,128)(2,1)S(1)}, u32[]{:S(2)}, u32[]{:S(2)}) collective-permute-start(bf16[528,256]{1,0:T(8,128)(2,1)} %get-tuple-element.97), channel_id=1, source_target_pairs={{2,4},{6,8},{10,12},{14,16},{18,20},{22,24},{26,28},{30,32},{34,36... | collective-permute-start | bytes 811016 | tf_op jit(solution)/shard_map/hop2O/ppermute | solution.py:201
  56.0 1.5 %copy-start.1 = (bf16[512,1024]{1,0:T(8,128)(2,1)S(1)}, bf16[512,1024]{1,0:T(8,128)(2,1)}, u32[]{:S(2)}) copy-start(bf16[512,1024]{1,0:T(8,128)(2,1)} %copy-done) | copy-start | bytes 3145732
  57.6 11.0 %copy-start.7 = (bf16[1024,256]{1,0:T(8,128)(2,1)S(1)}, bf16[1024,256]{1,0:T(8,128)(2,1)}, u32[]{:S(2)}) copy-start(bf16[1024,256]{1,0:T(8,128)(2,1)} %copy-done.6) | copy-start | bytes 1572868
  57.6 11.0 %copy-start.9 = (bf16[512,256]{1,0:T(8,128)(2,1)S(1)}, bf16[512,256]{1,0:T(8,128)(2,1)}, u32[]{:S(2)}) copy-start(bf16[512,256]{1,0:T(8,128)(2,1)} %copy-done.8) | copy-start | bytes 786436
  70.2 4.8 %copy-start.14 = (bf16[1024,1,1,256]{3,2,1,0:T(2,128)(2,1)S(1)}, bf16[1024,1,1,256]{3,2,1,0:T(2,128)(2,1)}, u32[]{:S(2)}) copy-start(bf16[1024,1,1,256]{3,2,1,0:T(2,128)(2,1)} %get-tuple-element.151) | copy-start | bytes 1572868
  70.3 17.3 %copy-start.3 = (f32[1024,512]{1,0:T(8,128)S(1)}, f32[1024,512]{1,0:T(8,128)}, u32[]{:S(2)}) copy-start(f32[1024,512]{1,0:T(8,128)} %loadings_ref.5) | copy-start | bytes 6291460
  70.9 16.8 %collective-permute-start.7 = (bf16[1024,512]{1,0:T(8,128)(2,1)S(1)}, bf16[1024,512]{1,0:T(8,128)(2,1)S(1)}, u32[]{:S(2)}, u32[]{:S(2)}) collective-permute-start(bf16[1024,512]{1,0:T(8,128)(2,1)S(1)} %get-tuple-element.110), channel_id=1, source_target_pairs={{0,1},{1,0},{2,3},{3,2},{4,5},{5,4},{6,7},{7,6},{8,9},{9,8},{10,11... | collective-permute-start | bytes 3145736 | tf_op jit(solution)/shard_map/swap_mid/ppermute | solution.py:204
  72.4 15.7 %collective-permute-start.8 = (bf16[528,256]{1,0:T(8,128)(2,1)S(1)}, bf16[528,256]{1,0:T(8,128)(2,1)S(1)}, u32[]{:S(2)}, u32[]{:S(2)}) collective-permute-start(bf16[528,256]{1,0:T(8,128)(2,1)S(1)} %get-tuple-element.113), channel_id=1, source_target_pairs={{2,4},{6,8},{10,12},{14,16},{18,20},{22,24},{26,28},{30,32},{34,36... | collective-permute-start | bytes 811016 | tf_op jit(solution)/shard_map/hop3E/ppermute | solution.py:201
  73.7 17.4 %collective-permute-start.6 = (bf16[528,256]{1,0:T(8,128)(2,1)S(1)}, bf16[528,256]{1,0:T(8,128)(2,1)S(1)}, u32[]{:S(2)}, u32[]{:S(2)}) collective-permute-start(bf16[528,256]{1,0:T(8,128)(2,1)S(1)} %get-tuple-element.105), channel_id=1, source_target_pairs={{0,2},{4,6},{8,10},{12,14},{16,18},{20,22},{24,26},{28,30},{32,34}... | collective-permute-start | bytes 811016 | tf_op jit(solution)/shard_map/hop3O/ppermute | solution.py:201
  89.8 3.8 %collective-permute-start.10 = (bf16[528,256]{1,0:T(8,128)(2,1)S(1)}, bf16[528,256]{1,0:T(8,128)(2,1)S(1)}, u32[]{:S(2)}, u32[]{:S(2)}) collective-permute-start(bf16[528,256]{1,0:T(8,128)(2,1)S(1)} %get-tuple-element.120), channel_id=1, source_target_pairs={{0,2},{4,6},{8,10},{12,14},{16,18},{20,22},{24,26},{28,30},{32,34}... | collective-permute-start | bytes 811016 | tf_op jit(solution)/shard_map/hop4E/ppermute | solution.py:201
  91.1 2.3 %copy-start.13 = (bf16[1024,1,1,256]{3,2,1,0:T(2,128)(2,1)S(1)}, bf16[1024,1,1,256]{3,2,1,0:T(2,128)(2,1)}, u32[]{:S(2)}) copy-start(bf16[1024,1,1,256]{3,2,1,0:T(2,128)(2,1)} %get-tuple-element.150) | copy-start | bytes 1572868
  92.1 13.5 %collective-permute-start.9 = (bf16[528,256]{1,0:T(8,128)(2,1)S(1)}, bf16[528,256]{1,0:T(8,128)(2,1)S(1)}, u32[]{:S(2)}, u32[]{:S(2)}) collective-permute-start(bf16[528,256]{1,0:T(8,128)(2,1)S(1)} %get-tuple-element.117), channel_id=1, source_target_pairs={{2,4},{6,8},{10,12},{14,16},{18,20},{22,24},{26,28},{30,32},{34,36... | collective-permute-start | bytes 811016 | tf_op jit(solution)/shard_map/hop4O/ppermute | solution.py:201
  94.1 15.6 %collective-permute-start.12 = (bf16[528,256]{1,0:T(8,128)(2,1)S(1)}, bf16[528,256]{1,0:T(8,128)(2,1)S(1)}, u32[]{:S(2)}, u32[]{:S(2)}) collective-permute-start(bf16[528,256]{1,0:T(8,128)(2,1)S(1)} %get-tuple-element.128), channel_id=1, source_target_pairs={{2,4},{6,8},{10,12},{14,16},{18,20},{22,24},{26,28},{30,32},{34,36... | collective-permute-start | bytes 811016 | tf_op jit(solution)/shard_map/hop5E/ppermute | solution.py:201
  105.6 3.0 %copy-start.12 = (bf16[1024,1,1,256]{3,2,1,0:T(2,128)(2,1)S(1)}, bf16[1024,1,1,256]{3,2,1,0:T(2,128)(2,1)}, u32[]{:S(2)}) copy-start(bf16[1024,1,1,256]{3,2,1,0:T(2,128)(2,1)} %get-tuple-element.149) | copy-start | bytes 1572868
  107.4 5.3 %collective-permute-start.11 = (bf16[528,256]{1,0:T(8,128)(2,1)S(1)}, bf16[528,256]{1,0:T(8,128)(2,1)S(1)}, u32[]{:S(2)}, u32[]{:S(2)}) collective-permute-start(bf16[528,256]{1,0:T(8,128)(2,1)S(1)} %get-tuple-element.125), channel_id=1, source_target_pairs={{0,2},{4,6},{8,10},{12,14},{16,18},{20,22},{24,26},{28,30},{32,34}... | collective-permute-start | bytes 811016 | tf_op jit(solution)/shard_map/hop5O/ppermute | solution.py:201
  111.4 4.3 %collective-permute-start.14 = (bf16[528,256]{1,0:T(8,128)(2,1)S(1)}, bf16[528,256]{1,0:T(8,128)(2,1)S(1)}, u32[]{:S(2)}, u32[]{:S(2)}) collective-permute-start(bf16[528,256]{1,0:T(8,128)(2,1)S(1)} %get-tuple-element.136), channel_id=1, source_target_pairs={{0,2},{4,6},{8,10},{12,14},{16,18},{20,22},{24,26},{28,30},{32,34}... | collective-permute-start | bytes 811016 | tf_op jit(solution)/shard_map/hop6E/ppermute | solution.py:201
  112.7 2.8 %copy-start.11 = (bf16[1024,1,1,256]{3,2,1,0:T(2,128)(2,1)S(1)}, bf16[1024,1,1,256]{3,2,1,0:T(2,128)(2,1)}, u32[]{:S(2)}) copy-start(bf16[1024,1,1,256]{3,2,1,0:T(2,128)(2,1)} %get-tuple-element.148) | copy-start | bytes 1572868
  114.2 13.6 %collective-permute-start.13 = (bf16[528,256]{1,0:T(8,128)(2,1)S(1)}, bf16[528,256]{1,0:T(8,128)(2,1)S(1)}, u32[]{:S(2)}, u32[]{:S(2)}) collective-permute-start(bf16[528,256]{1,0:T(8,128)(2,1)S(1)} %get-tuple-element.133), channel_id=1, source_target_pairs={{2,4},{6,8},{10,12},{14,16},{18,20},{22,24},{26,28},{30,32},{34,36... | collective-permute-start | bytes 811016 | tf_op jit(solution)/shard_map/hop6O/ppermute | solution.py:201
  130.1 17.4 %collective-permute-start.15 = (bf16[512,512]{1,0:T(8,128)(2,1)S(1)}, bf16[512,512]{1,0:T(8,128)(2,1)S(1)}, u32[]{:S(2)}, u32[]{:S(2)}) collective-permute-start(bf16[512,512]{1,0:T(8,128)(2,1)S(1)} %get-tuple-element.145), channel_id=1, source_target_pairs={{0,1},{1,0},{2,3},{3,2},{4,5},{5,4},{6,7},{7,6},{8,9},{9,8},{10,11... | collective-permute-start | bytes 1572872 | tf_op jit(solution)/shard_map/swap_end/ppermute | solution.py:204
  131.6 2.6 %collective-permute-start.17 = (bf16[528,256]{1,0:T(8,128)(2,1)S(1)}, bf16[528,256]{1,0:T(8,128)(2,1)S(1)}, u32[]{:S(2)}, u32[]{:S(2)}) collective-permute-start(bf16[528,256]{1,0:T(8,128)(2,1)S(1)} %get-tuple-element.147), channel_id=1, source_target_pairs={{0,2},{4,6},{8,10},{12,14},{16,18},{20,22},{24,26},{28,30},{32,34}... | collective-permute-start | bytes 811016 | tf_op jit(solution)/shard_map/hop7O/ppermute | solution.py:201
  132.9 13.5 %collective-permute-start.16 = (bf16[528,256]{1,0:T(8,128)(2,1)S(1)}, bf16[528,256]{1,0:T(8,128)(2,1)S(1)}, u32[]{:S(2)}, u32[]{:S(2)}) collective-permute-start(bf16[528,256]{1,0:T(8,128)(2,1)S(1)} %get-tuple-element.146), channel_id=1, source_target_pairs={{2,4},{6,8},{10,12},{14,16},{18,20},{22,24},{26,28},{30,32},{34,36... | collective-permute-start | bytes 811016 | tf_op jit(solution)/shard_map/hop7E/ppermute | solution.py:201
